TPU v7x, 128 devices: a whole 4x4x4 slice. The times are simulated.
128 devices in a mesh: grp: 8 (over x, core), tp: 16 (over z, y).
Axes of the slice: x: 4, y: 4, z: 4, core: 2. Of those that a mesh axis runs over, the one named last changes fastest.
Arguments:
- hidden_states: bfloat16 [2048, 8192], P('grp', 'tp'), may hold values from -6 to 6
- norm_gain: float32 [8192], replicated, may hold values from 0.5 to 1.5
- w_query: bfloat16 [8192, 8192], P(None, 'tp'), may hold values from -0.0625 to 0.0625
- w_key: bfloat16 [8192, 1024], P(None, 'tp'), may hold values from -0.0625 to 0.0625
- w_value: bfloat16 [8192, 1024], P(None, 'tp'), may hold values from -0.0625 to 0.0625
- cache: bfloat16 [16384, 2048], P('grp', 'tp'), may hold values from -82 to 82
- w_out: bfloat16 [8192, 8192], P('tp'), may hold values from -6 to 6
Outputs:
- mixed: bfloat16 [2048, 8192], P('grp', 'tp')
All inputs are finite; a program needn't handle non-finite values.
Results may differ from a plain program's by a relative error of at most 0.03.
Values may be sent and summed in bfloat16 or wider, within the bound.
A program may use at most 128 MiB of HBM per device.

v0:
```python
import math
import jax
import jax.numpy as jnp
from jax import lax
from jax.sharding import Mesh
from jax.sharding import PartitionSpec as P

HEAD_DIM = 128
TP = ("tp_0", "tp_1")


def swapped(array, axis, distance):
    return lax.ppermute(array, axis, [(i, i ^ 1 << distance) for i in range(lax.axis_size(axis))])


def from_everyone(array, axis):
    copies = jnp.broadcast_to(array, (lax.axis_size(axis), *array.shape))
    return lax.all_to_all(copies, axis, split_axis=0, concat_axis=0, tiled=True)


def in_order(pieces, dim):
    pieces = jnp.moveaxis(pieces, 0, dim)
    shape = pieces.shape
    return pieces.reshape(*shape[:dim], shape[dim] * shape[dim + 1], *shape[dim + 2 :])


def gather_directly(array, axis, dim):
    pieces = from_everyone(array, axis)
    return in_order(pieces, dim)


def sent_together(arrays, axis, split_dim, concat_dim, along):
    columns = [a.reshape(*a.shape[:along], -1) for a in arrays]
    both = jnp.concatenate(columns, axis=along)
    whole, at, done = (
        lax.all_to_all(both, axis, split_axis=split_dim, concat_axis=concat_dim, tiled=True),
        0,
        [],
    )
    for a, column in zip(arrays, columns):
        slab = whole[..., at : at + column.shape[along]]
        done.append(slab.reshape(*slab.shape[:along], *a.shape[along:]))
        at += column.shape[along]
    return tuple(done)


def sum_by_axis(terms, axes):
    total = terms.astype(jnp.bfloat16)
    for axis in axes:
        total = lax.psum_scatter(total, axis, scatter_dimension=0, tiled=True)
    return total.astype(jnp.float32)


def rotate(values, positions):
    half = values.shape[-1] // 2
    freqs = 500000.0 ** (-jnp.arange(half, dtype=jnp.float32) * 2.0 / values.shape[-1])
    angles = positions.astype(jnp.float32)[..., None] * freqs
    cosine = jnp.cos(angles)
    sine = jnp.sin(angles)
    first = values[..., :half]
    second = values[..., half:]
    return jnp.concatenate([first * cosine - second * sine, second * cosine + first * sine], -1)


def absorb(state, queries, keys, values, key_start, query_start, heads):
    count = keys.shape[0]
    block = math.gcd(count, 1024)
    steps = count // block
    width = keys.shape[1]
    scale = 1.0 / math.sqrt(width)
    query_pos = query_start + jnp.arange(queries.shape[0], dtype=jnp.int32) // heads

    def visit(carry, item):
        best, total, summed = carry
        key_block, value_block, index = item
        scores = (
            lax.dot_general(
                queries, key_block, (((1,), (1,)), ((), ())), preferred_element_type=jnp.float32
            )
            * scale
        )
        if key_start is not None:
            key_pos = key_start + index * block + jnp.arange(block, dtype=jnp.int32)
            scores = jnp.where(key_pos[None, :] <= query_pos[:, None], scores, -1e30)
        top = jnp.maximum(best, jnp.max(scores, axis=1))
        factor = jnp.exp(best - top)
        weights = jnp.exp(scores - top[:, None])
        total = total * factor + jnp.sum(weights, axis=1)
        summed = summed * factor[:, None] + jnp.dot(
            weights.astype(jnp.bfloat16), value_block, preferred_element_type=jnp.float32
        )
        return ((top, total, summed), None)

    result, unused = lax.scan(
        visit,
        state,
        (
            keys.reshape(steps, block, width),
            values.reshape(steps, block, width),
            jnp.arange(steps, dtype=jnp.int32),
        ),
    )
    return result


def body(hidden_states, norm_gain, w_query, w_key, w_value, cache, w_out):
    rows = hidden_states.shape[0]
    groups = lax.axis_size("grp")
    group = lax.axis_index("grp")
    parity = lax.axis_index(TP) % 2
    whole = lax.all_gather(hidden_states, TP, axis=1, tiled=True).astype(jnp.float32)
    normed = (
        whole * lax.rsqrt(jnp.mean(whole * whole, axis=1, keepdims=True) + 1e-05) * norm_gain
    ).astype(jnp.bfloat16)
    prefix = cache.shape[0] * groups
    first = group * rows
    positions = prefix + first + jnp.arange(rows, dtype=jnp.int32)
    heads = w_query.shape[1] // HEAD_DIM
    lanes = rows * heads
    query = jnp.dot(normed, w_query, preferred_element_type=jnp.float32).reshape(
        rows, heads, HEAD_DIM
    )
    query = rotate(query, positions[:, None]).astype(jnp.bfloat16).reshape(lanes, HEAD_DIM)
    key_part = jnp.dot(normed, w_key, preferred_element_type=jnp.float32)
    value_part = jnp.dot(normed, w_value, preferred_element_type=jnp.float32)
    partner_cache = swapped(cache, TP, 0)
    cache_key = jnp.where(parity == 0, cache, partner_cache)
    cache_value = jnp.where(parity == 0, partner_cache, cache)
    partner_key, partner_value = (
        swapped(key_part.astype(jnp.bfloat16), TP, 0).astype(key_part.dtype),
        swapped(value_part.astype(jnp.bfloat16), TP, 0).astype(value_part.dtype),
    )
    key_full = jnp.where(
        parity == 0,
        jnp.concatenate([key_part, partner_key], 1),
        jnp.concatenate([partner_key, key_part], 1),
    )
    value_full = jnp.where(
        parity == 0,
        jnp.concatenate([value_part, partner_value], 1),
        jnp.concatenate([partner_value, value_part], 1),
    )
    key_new = rotate(key_full, positions).astype(jnp.bfloat16)
    value_new = value_full.astype(jnp.bfloat16)
    start_state = (
        jnp.full((lanes,), -1e30, jnp.float32),
        jnp.zeros((lanes,), jnp.float32),
        jnp.zeros((lanes, HEAD_DIM), jnp.float32),
    )
    every = gather_directly(query, "grp", 0).reshape(groups, lanes, HEAD_DIM)

    def serve(item):
        block_queries, block_index = item
        state = absorb(
            start_state, block_queries, cache_key, cache_value, None, block_index * rows, heads
        )
        return absorb(state, block_queries, key_new, value_new, first, block_index * rows, heads)

    best, total, summed = lax.map(serve, (every, jnp.arange(groups, dtype=jnp.int32)))
    summed, best, total = tuple(
        (
            part.astype(jnp.float32)
            for part in sent_together(
                (
                    summed.astype(jnp.bfloat16),
                    best.astype(jnp.bfloat16),
                    total.astype(jnp.bfloat16),
                ),
                "grp",
                0,
                0,
                2,
            )
        )
    )
    top = jnp.max(best, axis=0)
    factor = jnp.exp(best - top[None, :])
    attended = (
        jnp.sum(summed * factor[:, :, None], axis=0) / jnp.sum(total * factor, axis=0)[:, None]
    )
    attended = attended.astype(jnp.bfloat16).reshape(rows, heads * HEAD_DIM)
    mixed = sum_by_axis(
        lax.dot_general(
            w_out, attended, (((0,), (1,)), ((), ())), preferred_element_type=jnp.float32
        ),
        TP,
    )
    return mixed.T.astype(jnp.bfloat16)


def solution(mesh):
    finer = Mesh(mesh.devices.reshape(mesh.shape["grp"], 4, 4), ("grp", "tp_0", "tp_1"))
    in_specs = (P("grp", TP), P(), P(None, TP), P(None, TP), P(None, TP), P("grp", TP), P(TP, None))
    out_specs = P("grp", TP)
    return jax.shard_map(body, mesh=finer, in_specs=in_specs, out_specs=out_specs, check_vma=False)
```

profile of v0, /device:TPU:0, one launch (start us, length us, event | category | flops | bytes accessed | tf_op | source)
XLA Modules:
  0.0 305.9 jit_solution(13559694169984585403)
XLA Ops:
  7.3 62.4 %all-gather.2.cloned.1.call-done = bf16[256,8192]{1,0:T(8,128)(2,1)} async-done(((bf16[256,512]{1,0:T(8,128)(2,1)}), bf16[256,8192]{1,0:T(8,128)(2,1)}) %all-gather.2.cloned.1.call-update) | async-done | bytes 4194320 | tf_op jit(solution)/shard_map/all_gather | solution.py:111
  69.7 3.3 %fusion.29 = f32[256]{0:T(256)S(1)} fusion(bf16[256,8192]{1,0:T(8,128)(2,1)} %all-gather.2.cloned.1.call-done), kind=kLoop, calls=%fused_computation.46 | loop fusion | flops 6291200 | bytes 4195328 | tf_op jit(solution)/shard_map/reduce_sum | solution.py:113
  73.2 1.5 fusion.49
  74.7 1.3 collective-permute-start.1
  76.5 2.4 fusion.45
  80.3 1.7 broadcast_in_dim.80
  82.0 4.3 %all-to-all-start = ((bf16[8,1024,128]{2,1,0:T(8,128)(2,1)}), bf16[8,1024,128]{2,1,0:T(8,128)(2,1)}, u32[]{:S(2)}, u32[]{:S(2)}) async-start(bf16[8,1024,128]{2,1,0:T(8,128)(2,1)} %broadcast_in_dim.80), calls=%async_computation | async-start | bytes 4194304 | tf_op jit(solution)/shard_map/all_to_all | solution.py:18
  86.4 1.3 collective-permute-start
  87.7 3.9 %fusion.41 = bf16[256,64]{0,1:T(8,128)(2,1)S(1)} fusion(bf16[8192,64]{0,1:T(8,128)(2,1)} %param.15, bf16[256,8192]{1,0:T(8,128)(2,1)} %all-gather.2.cloned.1.call-done, f32[8192]{0:T(1024)S(1)} %copy-done.4, f32[256]{0:T(256)S(1)} %add_rsqrt_fusion), kind=kOutput, calls=%fused_computation.81 | convolution fusion | flops 276824064 | bytes 5309440 | tf_op jit(solution)/shard_map/dot_general | solution.py:125
  91.6 1.1 collective-permute-start.2
  92.7 8.3 %collective-permute-done = bf16[2048,128]{1,0:T(8,128)(2,1)S(1)} collective-permute-done((bf16[2048,128]{1,0:T(8,128)(2,1)S(1)}, bf16[2048,128]{1,0:T(8,128)(2,1)S(1)}, u32[]{:S(2)}, u32[]{:S(2)}) %collective-permute-start) | collective-permute-done | bytes 524320 | tf_op jit(solution)/shard_map/ppermute | solution.py:13
  101.7 11.9 %all-to-all-done = bf16[8,1024,128]{2,1,0:T(8,128)(2,1)} async-done(((bf16[8,1024,128]{2,1,0:T(8,128)(2,1)}), bf16[8,1024,128]{2,1,0:T(8,128)(2,1)}, u32[]{:S(2)}, u32[]{:S(2)}) %all-to-all-start) | async-done | bytes 2097184 | tf_op jit(solution)/shard_map/all_to_all | solution.py:18
  113.6 73.2 %while.47 = (s32[]{:T(128)}, bf16[8,1024]{1,0:T(8,128)(2,1)S(1)}, bf16[8,1024]{1,0:T(8,128)(2,1)S(1)}, bf16[8,1024,128]{1,2,0:T(8,128)(2,1)}, bf16[2048,128]{1,0...) while((s32[]{:T(128)}, bf16[8,1024]{1,0:T(8,128)(2,1)S(1)}, ...), condition=%wide.region_8.9_spmd, body=%wide.region_1.8_spmd.sunk | while | flops 682377472 | bytes 20466068 | solution.py:159
  115.8 5.0 %while.48 = (s32[]{:T(128)}, f32[1024]{0:T(1024)S(1)}, f32[1024]{0:T(1024)S(1)}, f32[1024,128]{1,0:T(8,128)S(1)}, bf16[2,1024,128]{2,1,0:T(8,128)(2,1)S(1)}, /*i...) while((s32[]{:T(128)}, f32[1024]{0:T(1024)S(1)}, ...), condition=%wide.region_5.5_spmd.clone, body=%wide.region_2.4_spmd.clone.sunk | while | flops 545657856 | bytes 14483577 | solution.py:94
  117.3 1.0 fusion.85
  124.9 5.0 %while.48 = (s32[]{:T(128)}, f32[1024]{0:T(1024)S(1)}, f32[1024]{0:T(1024)S(1)}, f32[1024,128]{1,0:T(8,128)S(1)}, bf16[2,1024,128]{2,1,0:T(8,128)(2,1)S(1)}, /*i...) while((s32[]{:T(128)}, f32[1024]{0:T(1024)S(1)}, ...), condition=%wide.region_5.5_spmd.clone, body=%wide.region_2.4_spmd.clone.sunk | while | flops 545657856 | bytes 14483577 | solution.py:94
  126.4 1.0 fusion.85
  134.1 5.0 %while.48 = (s32[]{:T(128)}, f32[1024]{0:T(1024)S(1)}, f32[1024]{0:T(1024)S(1)}, f32[1024,128]{1,0:T(8,128)S(1)}, bf16[2,1024,128]{2,1,0:T(8,128)(2,1)S(1)}, /*i...) while((s32[]{:T(128)}, f32[1024]{0:T(1024)S(1)}, ...), condition=%wide.region_5.5_spmd.clone, body=%wide.region_2.4_spmd.clone.sunk | while | flops 545657856 | bytes 14483577 | solution.py:94
  143.2 5.0 %while.48 = (s32[]{:T(128)}, f32[1024]{0:T(1024)S(1)}, f32[1024]{0:T(1024)S(1)}, f32[1024,128]{1,0:T(8,128)S(1)}, bf16[2,1024,128]{2,1,0:T(8,128)(2,1)S(1)}, /*i...) while((s32[]{:T(128)}, f32[1024]{0:T(1024)S(1)}, ...), condition=%wide.region_5.5_spmd.clone, body=%wide.region_2.4_spmd.clone.sunk | while | flops 545657856 | bytes 14483577 | solution.py:94
  144.7 1.0 fusion.85
  152.4 5.0 %while.48 = (s32[]{:T(128)}, f32[1024]{0:T(1024)S(1)}, f32[1024]{0:T(1024)S(1)}, f32[1024,128]{1,0:T(8,128)S(1)}, bf16[2,1024,128]{2,1,0:T(8,128)(2,1)S(1)}, /*i...) while((s32[]{:T(128)}, f32[1024]{0:T(1024)S(1)}, ...), condition=%wide.region_5.5_spmd.clone, body=%wide.region_2.4_spmd.clone.sunk | while | flops 545657856 | bytes 14483577 | solution.py:94
  153.9 1.0 fusion.85
  156.4 1.0 fusion.85
  161.5 5.0 %while.48 = (s32[]{:T(128)}, f32[1024]{0:T(1024)S(1)}, f32[1024]{0:T(1024)S(1)}, f32[1024,128]{1,0:T(8,128)S(1)}, bf16[2,1024,128]{2,1,0:T(8,128)(2,1)S(1)}, /*i...) while((s32[]{:T(128)}, f32[1024]{0:T(1024)S(1)}, ...), condition=%wide.region_5.5_spmd.clone, body=%wide.region_2.4_spmd.clone.sunk | while | flops 545657856 | bytes 14483577 | solution.py:94
  170.7 5.0 %while.48 = (s32[]{:T(128)}, f32[1024]{0:T(1024)S(1)}, f32[1024]{0:T(1024)S(1)}, f32[1024,128]{1,0:T(8,128)S(1)}, bf16[2,1024,128]{2,1,0:T(8,128)(2,1)S(1)}, /*i...) while((s32[]{:T(128)}, f32[1024]{0:T(1024)S(1)}, ...), condition=%wide.region_5.5_spmd.clone, body=%wide.region_2.4_spmd.clone.sunk | while | flops 545657856 | bytes 14483577 | solution.py:94
  179.8 5.0 %while.48 = (s32[]{:T(128)}, f32[1024]{0:T(1024)S(1)}, f32[1024]{0:T(1024)S(1)}, f32[1024,128]{1,0:T(8,128)S(1)}, bf16[2,1024,128]{2,1,0:T(8,128)(2,1)S(1)}, /*i...) while((s32[]{:T(128)}, f32[1024]{0:T(1024)S(1)}, ...), condition=%wide.region_5.5_spmd.clone, body=%wide.region_2.4_spmd.clone.sunk | while | flops 545657856 | bytes 14483577 | solution.py:94
  183.8 1.0 fusion.85
  186.8 1.9 pad_maximum_fusion
  188.7 31.3 %all_to_all.10 = bf16[8,1024,130]{1,2,0:T(8,128)(2,1)S(1)} all-to-all(bf16[8,1024,130]{1,2,0:T(8,128)(2,1)S(1)} %pad_maximum_fusion), channel_id=1, replica_groups=mesh['grp'=8,'tp_0'=4,'tp_1'=4] {'grp'}, dimensions={0} | all-to-all | bytes 4259840 | tf_op jit(solution)/shard_map/all_to_all | solution.py:36
  221.4 7.7 %fusion.28 = bf16[8192,256]{0,1:T(8,128)(2,1)} fusion(bf16[512,8192]{1,0:T(8,128)(2,1)} %param.17, f32[256,512]{1,0:T(8,128)S(1)} %reduce_sum.54, f32[32,8,4,128]{3,2,1,0:T(4,128)S(1)} %bitcast.92), kind=kOutput, calls=%fused_computation.45 | convolution fusion | flops 2149842944 | bytes 13631488 | tf_op jit(solution)/shard_map/dot_general | solution.py:183
  229.2 44.6 %reduce-scatter.3.cloned.1.call-done = bf16[2048,256]{0,1:T(8,128)(2,1)} async-done(((bf16[8192,256]{0,1:T(8,128)(2,1)}), bf16[2048,256]{0,1:T(8,128)(2,1)}) %reduce-scatter.3.cloned.1.call-update) | async-done | bytes 1048592 | tf_op jit(solution)/shard_map/reduce_scatter | solution.py:50
  273.8 25.7 %reduce-scatter.5.cloned.1.call-done = bf16[512,256]{0,1:T(8,128)(2,1)} async-done(((bf16[2048,256]{0,1:T(8,128)(2,1)}), bf16[512,256]{0,1:T(8,128)(2,1)}) %reduce-scatter.5.cloned.1.call-update) | async-done | bytes 262160 | tf_op jit(solution)/shard_map/reduce_scatter | solution.py:50
  (267 shorter events, 66.1 us)
Async XLA Ops:
  6.5 66.4 %copy-start = (bf16[8192,64]{0,1:T(8,128)(2,1)S(1)}, bf16[8192,64]{0,1:T(8,128)(2,1)}, u32[]{:S(2)}) copy-start(bf16[8192,64]{0,1:T(8,128)(2,1)} %param.14) | copy-start | bytes 3145732
  6.5 66.4 %copy-start.4 = (f32[8192]{0:T(1024)S(1)}, f32[8192]{0:T(1024)}, u32[]{:S(2)}) copy-start(f32[8192]{0:T(1024)} %param.12) | copy-start | bytes 98308
  6.5 63.2 %all-gather.2.cloned.1.call-start = ((), (), s32[]{:S(2)}) async-start(), calls=%async_computation.4 | async-start | bytes 4456448 | tf_op jit(solution)/shard_map/all_gather | solution.py:111
  69.7 3.4 %copy-start.1 = (bf16[256,8192]{1,0:T(8,128)(2,1)S(1)}, bf16[256,8192]{1,0:T(8,128)(2,1)}, u32[]{:S(2)}) copy-start(bf16[256,8192]{1,0:T(8,128)(2,1)} %all-gather.2.cloned.1.call-done) | copy-start | bytes 12582916
  73.1 3.4 %copy-start.3 = (bf16[8192,512]{1,0:T(8,128)(2,1)S(1)}, bf16[8192,512]{1,0:T(8,128)(2,1)}, u32[]{:S(2)}) copy-start(bf16[8192,512]{1,0:T(8,128)(2,1)} %param.13) | copy-start | bytes 25165828
  74.7 4.4 %collective-permute-start.1 = (bf16[256,64]{0,1:T(8,128)(2,1)S(1)}, bf16[256,64]{0,1:T(8,128)(2,1)S(1)}, u32[]{:S(2)}, u32[]{:S(2)}) collective-permute-start(bf16[256,64]{0,1:T(8,128)(2,1)S(1)} %get-tuple-element.383), channel_id=1, source_target_pairs={{0,1},{1,0},{2,3},{3,2},{4,5},{5,4},{6,7},{7,6},{8,9},{9,8},{10,11... | collective-permute-start | bytes 98312 | tf_op jit(solution)/shard_map/ppermute | solution.py:13
  79.7 6.7 %copy-start.2 = (bf16[2048,128]{1,0:T(8,128)(2,1)S(1)}, bf16[2048,128]{1,0:T(8,128)(2,1)}, u32[]{:S(2)}) copy-start(bf16[2048,128]{1,0:T(8,128)(2,1)} %param.16) | copy-start | bytes 1572868
  82.0 31.6 %all-to-all-start = ((bf16[8,1024,128]{2,1,0:T(8,128)(2,1)}), bf16[8,1024,128]{2,1,0:T(8,128)(2,1)}, u32[]{:S(2)}, u32[]{:S(2)}) async-start(bf16[8,1024,128]{2,1,0:T(8,128)(2,1)} %broadcast_in_dim.80), calls=%async_computation | async-start | bytes 4194304 | tf_op jit(solution)/shard_map/all_to_all | solution.py:18
  86.4 187.4 %reduce-scatter.3.cloned.1.call-start = ((), (), s32[]{:S(2)}) async-start(), calls=%async_computation.5 | async-start | bytes 5242880 | tf_op jit(solution)/shard_map/reduce_scatter | solution.py:50
  86.4 14.6 %collective-permute-start = (bf16[2048,128]{1,0:T(8,128)(2,1)S(1)}, bf16[2048,128]{1,0:T(8,128)(2,1)S(1)}, u32[]{:S(2)}, u32[]{:S(2)}) collective-permute-start(bf16[2048,128]{1,0:T(8,128)(2,1)S(1)} %copy-done.2), channel_id=1, source_target_pairs={{0,1},{1,0},{2,3},{3,2},{4,5},{5,4},{6,7},{7,6},{8,9},{9,8},{10,11... | collective-permute-start | bytes 1572872 | tf_op jit(solution)/shard_map/ppermute | solution.py:13
  91.6 9.8 %collective-permute-start.2 = (bf16[256,64]{0,1:T(8,128)(2,1)S(1)}, bf16[256,64]{0,1:T(8,128)(2,1)S(1)}, u32[]{:S(2)}, u32[]{:S(2)}) collective-permute-start(bf16[256,64]{0,1:T(8,128)(2,1)S(1)} %fusion.41), channel_id=1, source_target_pairs={{0,1},{1,0},{2,3},{3,2},{4,5},{5,4},{6,7},{7,6},{8,9},{9,8},{10,11... | collective-permute-start | bytes 98312 | tf_op jit(solution)/shard_map/ppermute | solution.py:13
  229.1 70.3 %reduce-scatter.5.cloned.1.call-start = ((), (), s32[]{:S(2)}) async-start(), calls=%async_computation.6 | async-start | bytes 1310720 | tf_op jit(solution)/shard_map/reduce_scatter | solution.py:50
Sparse Core Ops, SparseCore 0:
  9.5 60.1 all-gather.1
  229.2 44.4 reduce-scatter.2
  276.3 23.0 reduce-scatter.4
where the time goes:
time: 307 us; the launch traced here: 306 us
  waiting for transfers between devices  154 us (50%)
  matrix products  48.3 us (16%)
  blocking collectives  31.3 us (10%)
  local copies, waits for them, and re-layouts  24.4 us (8%)
  other arithmetic  20.5 us (7%)
  between operations  13.4 us (4%)
  starting transfers between devices  8.07 us (3%)
  loops' own time  6.1 us (2%)
    reduce_scatter x2, waiting for transfers between devices, sum_by_axis(): total = lax.psum_scatter(total, axis, scatter_dimension=0, tiled=True)  70.2 us
    all_gather x1, waiting for transfers between devices, body(): lax.all_gather(hidden_states, TP, axis=1, tiled=True).astype(jnp.float32)  62.4 us
    all_to_all x1, blocking collectives, sent_together(): lax.all_to_all(both, axis, split_axis=split_dim, concat_axis=concat_dim,...  31.3 us
    dot_general x24, matrix products, visit(): jnp.dot(weights.astype(jnp.bfloat16), value_block, preferred_element_type...  18.8 us
    dot_general x24, matrix products, visit(): lax.dot_general(queries, key_block, (((1,), (1,)), ((), ())), preferred_e...  14 us
    reduce_sum x24, other arithmetic, visit(): total = total * factor + jnp.sum(weights, axis=1)  13.1 us
    all_to_all x1, waiting for transfers between devices, from_everyone(): return lax.all_to_all(copies, axis, split_axis=0, concat_axis=0, tiled=True)  11.9 us
    ppermute x3, waiting for transfers between devices, swapped(): lax.ppermute(array, axis, [(i, i ^ 1 << distance) for i in range(lax.axis...  8.59 us
  transfers between devices with their start and end apart: 7, of which 6 were waited for; matrix products, arithmetic and copies ran while one was open for 2% of the time, Pallas kernels for 0%

commit v1 on v0

--- a/solution.py
+++ b/solution.py
@@ -1,12 +1,30 @@
+import functools
 import math
 import jax
 import jax.numpy as jnp
 from jax import lax
 from jax.sharding import Mesh
 from jax.sharding import PartitionSpec as P
+from jax.lax import all_to_all, axis_size
 
 HEAD_DIM = 128
 TP = ("tp_0", "tp_1")
+
+
+def cut_spot(u_in, named_axis):
+    answer = jnp.concatenate(
+        all_to_all(
+            jnp.stack([u_in for _ in range(axis_size(named_axis))]),
+            axis_name=named_axis,
+            split_axis=0,
+            concat_axis=0,
+        ),
+        axis=1,
+    )
+    return answer
+
+
+deliver_task_by_axis = functools.partial(cut_spot, named_axis=TP)
 
 
 def swapped(array, axis, distance):
@@ -108,7 +126,7 @@
     groups = lax.axis_size("grp")
     group = lax.axis_index("grp")
     parity = lax.axis_index(TP) % 2
-    whole = lax.all_gather(hidden_states, TP, axis=1, tiled=True).astype(jnp.float32)
+    whole = deliver_task_by_axis(hidden_states).astype(jnp.float32)
     normed = (
         whole * lax.rsqrt(jnp.mean(whole * whole, axis=1, keepdims=True) + 1e-05) * norm_gain
     ).astype(jnp.bfloat16)

time: 307 us -> 402 us (1.31)
  other arithmetic: 20.5 us -> 60.3 us
  matrix products: 48.3 us -> 77.6 us
  local copies, waits for them, and re-layouts: 24.4 us -> 52.9 us
  waiting for transfers between devices: 154 us -> 143 us
  starting transfers between devices: 8.07 us -> 15.2 us
    all_gather x1 -> x0, waiting for transfers between devices: 62.4 us -> none  [body(): lax.all_gather(hidden_states, TP, axis=1, tiled=True).astype(jnp.float32)]
    all_to_all x0 -> x1, waiting for transfers between devices: none -> 51.4 us  [cut_spot(): all_to_all(jnp.stack([u_in for _ in range(axis_size(named_axis))]), axis_...]
    reduce_sum x24, other arithmetic: 13.1 us -> 50.6 us  [visit(): total = total * factor + jnp.sum(weights, axis=1)]
    dot_general x24, matrix products: 14 us -> 44.9 us  [visit(): lax.dot_general(queries, key_block, (((1,), (1,)), ((), ())), preferred_e...]
    dot_general x0 -> x1, local copies, waits for them, and re-layouts: none -> 11.7 us  [body(): jnp.dot(normed, w_query, preferred_element_type=jnp.float32)]
    all_to_all x0 -> x1, starting transfers between devices: none -> 8.31 us  [cut_spot(): all_to_all(jnp.stack([u_in for _ in range(axis_size(named_axis))]), axis_...]
    all_to_all x0 -> x1, local copies, waits for them, and re-layouts: none -> 6.36 us  [cut_spot(): all_to_all(jnp.stack([u_in for _ in range(axis_size(named_axis))]), axis_...]
    while x16 -> x48, local copies, waits for them, and re-layouts: 0.04 us -> 5.76 us
  transfers between devices with their start and end apart: 7 -> 7, of which waited for: 6 -> 6; matrix products, arithmetic and copies ran while one was open for 2% -> 5% of each run, Pallas kernels for 0% -> 0%
where the time goes in v1:
time: 402 us; the launch traced here: 401 us
  waiting for transfers between devices  143 us (36%)
  matrix products  77.6 us (19%)
  other arithmetic  60.3 us (15%)
  local copies, waits for them, and re-layouts  52.9 us (13%)
  blocking collectives  31.3 us (8%)
  starting transfers between devices  15.2 us (4%)
  between operations  13.8 us (3%)
  loops' own time  6.96 us (2%)
    reduce_scatter x2, waiting for transfers between devices, sum_by_axis(): total = lax.psum_scatter(total, axis, scatter_dimension=0, tiled=True)  69.8 us
    all_to_all x1, waiting for transfers between devices, cut_spot(): all_to_all(jnp.stack([u_in for _ in range(axis_size(named_axis))]), axis_...  51.4 us
    reduce_sum x24, other arithmetic, visit(): total = total * factor + jnp.sum(weights, axis=1)  50.6 us
    dot_general x24, matrix products, visit(): lax.dot_general(queries, key_block, (((1,), (1,)), ((), ())), preferred_e...  44.9 us
    all_to_all x1, blocking collectives, sent_together(): lax.all_to_all(both, axis, split_axis=split_dim, concat_axis=concat_dim,...  31.3 us
    dot_general x24, matrix products, visit(): jnp.dot(weights.astype(jnp.bfloat16), value_block, preferred_element_type...  18.8 us
    all_to_all x1, waiting for transfers between devices, from_everyone(): return lax.all_to_all(copies, axis, split_axis=0, concat_axis=0, tiled=True)  11.9 us
    dot_general x1, local copies, waits for them, and re-layouts, body(): jnp.dot(normed, w_query, preferred_element_type=jnp.float32)  11.7 us
  transfers between devices with their start and end apart: 7, of which 6 were waited for; matrix products, arithmetic and copies ran while one was open for 5% of the time, Pallas kernels for 0%

profile of v1, /device:TPU:0, one launch (start us, length us, event | category | flops | bytes accessed | tf_op | source)
XLA Modules:
  0.0 400.8 jit_solution(12619312428238322808)
XLA Ops:
  6.5 3.4 stack.2
  9.9 8.3 %all-to-all-start = ((bf16[16,256,512]{2,1,0:T(8,128)(2,1)}), bf16[16,256,512]{2,1,0:T(8,128)(2,1)}, u32[]{:S(2)}, u32[]{:S(2)}) async-start(bf16[16,256,512]{2,1,0:T(8,128)(2,1)} %stack.2), calls=%async_computation | async-start | bytes 8388608 | tf_op jit(solution)/shard_map/all_to_all | solution.py:16
  18.3 11.7 %copy.45 = bf16[512,8192]{1,0:T(8,128)(2,1)} copy(bf16[512,8192]{0,1:T(8,128)(2,1)} %bitcast.107) | data formatting | bytes 16777216 | tf_op jit(solution)/shard_map/dot_general | solution.py:138
  30.1 51.4 %all-to-all-done = bf16[16,256,512]{2,1,0:T(8,128)(2,1)} async-done(((bf16[16,256,512]{2,1,0:T(8,128)(2,1)}), bf16[16,256,512]{2,1,0:T(8,128)(2,1)}, u32[]{:S(2)}, u32[]{:S(2)}) %all-to-all-start) | async-done | bytes 4194336 | tf_op jit(solution)/shard_map/all_to_all | solution.py:16
  81.5 6.4 %copy.29 = bf16[16,256,512]{1,2,0:T(8,128)(2,1)} copy(bf16[16,256,512]{2,1,0:T(8,128)(2,1)} %all-to-all-done) | data formatting | bytes 8388608 | tf_op jit(solution)/shard_map/all_to_all | solution.py:16
  87.8 3.5 multiply_reduce_fusion.1
  101.5 4.4 %all-to-all-start.1 = ((bf16[8,1024,128]{2,1,0:T(8,128)(2,1)}), bf16[8,1024,128]{2,1,0:T(8,128)(2,1)}, u32[]{:S(2)}, u32[]{:S(2)}) async-start(bf16[8,1024,128]{2,1,0:T(8,128)(2,1)} %broadcast_in_dim.80), calls=%async_computation.1 | async-start | bytes 4194304 | tf_op jit(solution)/shard_map/all_to_all | solution.py:36
  111.3 9.3 %collective-permute-done = bf16[2048,128]{1,0:T(8,128)(2,1)S(1)} collective-permute-done((bf16[2048,128]{1,0:T(8,128)(2,1)S(1)}, bf16[2048,128]{1,0:T(8,128)(2,1)S(1)}, u32[]{:S(2)}, u32[]{:S(2)}) %collective-permute-start) | collective-permute-done | bytes 524320 | tf_op jit(solution)/shard_map/ppermute | solution.py:31
  121.2 11.9 %all-to-all-done.1 = bf16[8,1024,128]{2,1,0:T(8,128)(2,1)} async-done(((bf16[8,1024,128]{2,1,0:T(8,128)(2,1)}), bf16[8,1024,128]{2,1,0:T(8,128)(2,1)}, u32[]{:S(2)}, u32[]{:S(2)}) %all-to-all-start.1) | async-done | bytes 2097184 | tf_op jit(solution)/shard_map/all_to_all | solution.py:36
  133.1 148.5 %while.47 = (s32[]{:T(128)}, bf16[8,1024]{1,0:T(8,128)(2,1)S(1)}, bf16[8,1024]{1,0:T(8,128)(2,1)S(1)}, bf16[8,1024,128]{1,2,0:T(8,128)(2,1)}, bf16[2048,128]{1,0...) while((s32[]{:T(128)}, bf16[8,1024]{1,0:T(8,128)(2,1)S(1)}, ...), condition=%wide.region_8.9_spmd, body=%wide.region_1.8_spmd.sunk | while | flops 682377472 | bytes 37243804 | solution.py:177
  135.8 14.2 %while.48 = (s32[]{:T(128)}, f32[1024]{0:T(1024)S(1)}, f32[1024]{0:T(1024)S(1)}, f32[1024,128]{1,0:T(8,128)S(1)}, bf16[2,1024,128]{2,1,0:T(8,128)(2,1)S(1)}, /*i...) while((s32[]{:T(128)}, f32[1024]{0:T(1024)S(1)}, ...), condition=%wide.region_5.5_spmd.clone, body=%wide.region_2.4_spmd.clone.sunk | while | flops 545657856 | bytes 31260812 | solution.py:112
  138.5 3.1 fusion.81
  145.6 3.1 fusion.81
  154.4 14.2 %while.48 = (s32[]{:T(128)}, f32[1024]{0:T(1024)S(1)}, f32[1024]{0:T(1024)S(1)}, f32[1024,128]{1,0:T(8,128)S(1)}, bf16[2,1024,128]{2,1,0:T(8,128)(2,1)S(1)}, /*i...) while((s32[]{:T(128)}, f32[1024]{0:T(1024)S(1)}, ...), condition=%wide.region_5.5_spmd.clone, body=%wide.region_2.4_spmd.clone.sunk | while | flops 545657856 | bytes 31260812 | solution.py:112
  157.0 3.1 fusion.81
  164.1 3.1 fusion.81
  172.9 14.2 %while.48 = (s32[]{:T(128)}, f32[1024]{0:T(1024)S(1)}, f32[1024]{0:T(1024)S(1)}, f32[1024,128]{1,0:T(8,128)S(1)}, bf16[2,1024,128]{2,1,0:T(8,128)(2,1)S(1)}, /*i...) while((s32[]{:T(128)}, f32[1024]{0:T(1024)S(1)}, ...), condition=%wide.region_5.5_spmd.clone, body=%wide.region_2.4_spmd.clone.sunk | while | flops 545657856 | bytes 31260812 | solution.py:112
  175.6 3.1 fusion.81
  182.7 3.1 fusion.81
  191.5 14.2 %while.48 = (s32[]{:T(128)}, f32[1024]{0:T(1024)S(1)}, f32[1024]{0:T(1024)S(1)}, f32[1024,128]{1,0:T(8,128)S(1)}, bf16[2,1024,128]{2,1,0:T(8,128)(2,1)S(1)}, /*i...) while((s32[]{:T(128)}, f32[1024]{0:T(1024)S(1)}, ...), condition=%wide.region_5.5_spmd.clone, body=%wide.region_2.4_spmd.clone.sunk | while | flops 545657856 | bytes 31260812 | solution.py:112
  194.2 3.1 fusion.81
  201.3 3.1 fusion.81
  210.0 14.2 %while.48 = (s32[]{:T(128)}, f32[1024]{0:T(1024)S(1)}, f32[1024]{0:T(1024)S(1)}, f32[1024,128]{1,0:T(8,128)S(1)}, bf16[2,1024,128]{2,1,0:T(8,128)(2,1)S(1)}, /*i...) while((s32[]{:T(128)}, f32[1024]{0:T(1024)S(1)}, ...), condition=%wide.region_5.5_spmd.clone, body=%wide.region_2.4_spmd.clone.sunk | while | flops 545657856 | bytes 31260812 | solution.py:112
  212.7 3.1 fusion.81
  219.8 3.1 fusion.81
  228.6 14.2 %while.48 = (s32[]{:T(128)}, f32[1024]{0:T(1024)S(1)}, f32[1024]{0:T(1024)S(1)}, f32[1024,128]{1,0:T(8,128)S(1)}, bf16[2,1024,128]{2,1,0:T(8,128)(2,1)S(1)}, /*i...) while((s32[]{:T(128)}, f32[1024]{0:T(1024)S(1)}, ...), condition=%wide.region_5.5_spmd.clone, body=%wide.region_2.4_spmd.clone.sunk | while | flops 545657856 | bytes 31260812 | solution.py:112
  247.1 14.2 %while.48 = (s32[]{:T(128)}, f32[1024]{0:T(1024)S(1)}, f32[1024]{0:T(1024)S(1)}, f32[1024,128]{1,0:T(8,128)S(1)}, bf16[2,1024,128]{2,1,0:T(8,128)(2,1)S(1)}, /*i...) while((s32[]{:T(128)}, f32[1024]{0:T(1024)S(1)}, ...), condition=%wide.region_5.5_spmd.clone, body=%wide.region_2.4_spmd.clone.sunk | while | flops 545657856 | bytes 31260812 | solution.py:112
  265.7 14.2 %while.48 = (s32[]{:T(128)}, f32[1024]{0:T(1024)S(1)}, f32[1024]{0:T(1024)S(1)}, f32[1024,128]{1,0:T(8,128)S(1)}, bf16[2,1024,128]{2,1,0:T(8,128)(2,1)S(1)}, /*i...) while((s32[]{:T(128)}, f32[1024]{0:T(1024)S(1)}, ...), condition=%wide.region_5.5_spmd.clone, body=%wide.region_2.4_spmd.clone.sunk | while | flops 545657856 | bytes 31260812 | solution.py:112
  283.6 31.3 %all_to_all.15 = bf16[8,1024,130]{1,2,0:T(8,128)(2,1)S(1)} all-to-all(bf16[8,1024,130]{1,2,0:T(8,128)(2,1)S(1)} %pad_maximum_fusion), channel_id=1, replica_groups=mesh['grp'=8,'tp_0'=4,'tp_1'=4] {'grp'}, dimensions={0} | all-to-all | bytes 4259840 | tf_op jit(solution)/shard_map/all_to_all | solution.py:54
  316.2 7.8 %fusion.28 = bf16[8192,256]{0,1:T(8,128)(2,1)} fusion(bf16[512,8192]{1,0:T(8,128)(2,1)} %param.17, f32[256,512]{1,0:T(8,128)S(1)} %reduce_sum.54, f32[32,8,4,128]{3,2,1,0:T(4,128)S(1)} %bitcast.115), kind=kOutput, calls=%fused_computation.43 | convolution fusion | flops 2149842944 | bytes 13631488 | tf_op jit(solution)/shard_map/dot_general | solution.py:201
  324.1 44.2 %reduce-scatter.3.cloned.1.call-done = bf16[2048,256]{0,1:T(8,128)(2,1)} async-done(((bf16[8192,256]{0,1:T(8,128)(2,1)}), bf16[2048,256]{0,1:T(8,128)(2,1)}) %reduce-scatter.3.cloned.1.call-update) | async-done | bytes 1048592 | tf_op jit(solution)/shard_map/reduce_scatter | solution.py:68
  368.3 25.6 %reduce-scatter.5.cloned.1.call-done = bf16[512,256]{0,1:T(8,128)(2,1)} async-done(((bf16[2048,256]{0,1:T(8,128)(2,1)}), bf16[512,256]{0,1:T(8,128)(2,1)}) %reduce-scatter.5.cloned.1.call-update) | async-done | bytes 262160 | tf_op jit(solution)/shard_map/reduce_scatter | solution.py:68
  (312 shorter events, 130.2 us)
Async XLA Ops:
  6.5 86.0 %copy-start = (bf16[8192,64]{0,1:T(8,128)(2,1)S(1)}, bf16[8192,64]{0,1:T(8,128)(2,1)}, u32[]{:S(2)}) copy-start(bf16[8192,64]{0,1:T(8,128)(2,1)} %param.14) | copy-start | bytes 3145732
  9.9 8.3 %copy-start.7 = (f32[8192]{0:T(1024)S(1)}, f32[8192]{0:T(1024)}, u32[]{:S(2)}) copy-start(f32[8192]{0:T(1024)} %param.12) | copy-start | bytes 98308
  9.9 71.5 %all-to-all-start = ((bf16[16,256,512]{2,1,0:T(8,128)(2,1)}), bf16[16,256,512]{2,1,0:T(8,128)(2,1)}, u32[]{:S(2)}, u32[]{:S(2)}) async-start(bf16[16,256,512]{2,1,0:T(8,128)(2,1)} %stack.2), calls=%async_computation | async-start | bytes 8388608 | tf_op jit(solution)/shard_map/all_to_all | solution.py:16
  87.8 3.5 copy-start.3
  91.3 3.6 slice-start
  92.6 2.3 copy-start.4
  92.6 3.9 slice-start.1
  93.4 5.5 %collective-permute-start.1 = (bf16[256,64]{0,1:T(8,128)(2,1)S(1)}, bf16[256,64]{0,1:T(8,128)(2,1)S(1)}, u32[]{:S(2)}, u32[]{:S(2)}) collective-permute-start(bf16[256,64]{0,1:T(8,128)(2,1)S(1)} %get-tuple-element.383), channel_id=1, source_target_pairs={{0,1},{1,0},{2,3},{3,2},{4,5},{5,4},{6,7},{7,6},{8,9},{9,8},{10,11... | collective-permute-start | bytes 98312 | tf_op jit(solution)/shard_map/ppermute | solution.py:31
  99.3 6.6 %copy-start.6 = (bf16[2048,128]{1,0:T(8,128)(2,1)S(1)}, bf16[2048,128]{1,0:T(8,128)(2,1)}, u32[]{:S(2)}) copy-start(bf16[2048,128]{1,0:T(8,128)(2,1)} %param.16) | copy-start | bytes 1572868
  99.3 7.1 %copy-start.5 = (bf16[8192,64]{0,1:T(8,128)(2,1)S(1)}, bf16[8192,64]{0,1:T(8,128)(2,1)}, u32[]{:S(2)}) copy-start(bf16[8192,64]{0,1:T(8,128)(2,1)} %param.15) | copy-start | bytes 3145732
  101.5 31.6 %all-to-all-start.1 = ((bf16[8,1024,128]{2,1,0:T(8,128)(2,1)}), bf16[8,1024,128]{2,1,0:T(8,128)(2,1)}, u32[]{:S(2)}, u32[]{:S(2)}) async-start(bf16[8,1024,128]{2,1,0:T(8,128)(2,1)} %broadcast_in_dim.80), calls=%async_computation.1 | async-start | bytes 4194304 | tf_op jit(solution)/shard_map/all_to_all | solution.py:36
  105.9 262.4 %reduce-scatter.3.cloned.1.call-start = ((), (), s32[]{:S(2)}) async-start(), calls=%async_computation.5 | async-start | bytes 5242880 | tf_op jit(solution)/shard_map/reduce_scatter | solution.py:68
  105.9 14.6 %collective-permute-start = (bf16[2048,128]{1,0:T(8,128)(2,1)S(1)}, bf16[2048,128]{1,0:T(8,128)(2,1)S(1)}, u32[]{:S(2)}, u32[]{:S(2)}) collective-permute-start(bf16[2048,128]{1,0:T(8,128)(2,1)S(1)} %copy-done.6), channel_id=1, source_target_pairs={{0,1},{1,0},{2,3},{3,2},{4,5},{5,4},{6,7},{7,6},{8,9},{9,8},{10,11... | collective-permute-start | bytes 1572872 | tf_op jit(solution)/shard_map/ppermute | solution.py:31
  109.5 11.5 %collective-permute-start.2 = (bf16[256,64]{0,1:T(8,128)(2,1)S(1)}, bf16[256,64]{0,1:T(8,128)(2,1)S(1)}, u32[]{:S(2)}, u32[]{:S(2)}) collective-permute-start(bf16[256,64]{0,1:T(8,128)(2,1)S(1)} %fusion.44), channel_id=1, source_target_pairs={{0,1},{1,0},{2,3},{3,2},{4,5},{5,4},{6,7},{7,6},{8,9},{9,8},{10,11... | collective-permute-start | bytes 98312 | tf_op jit(solution)/shard_map/ppermute | solution.py:31
  138.5 3.4 copy-start.2
  145.6 3.4 copy-start.2
  157.0 3.4 copy-start.2
  164.1 3.4 copy-start.2
  175.6 3.4 copy-start.2
  182.7 3.4 copy-start.2
  194.1 3.4 copy-start.2
  201.3 3.4 copy-start.2
  212.7 3.4 copy-start.2
  219.8 3.4 copy-start.2
  231.3 3.4 copy-start.2
  238.4 3.4 copy-start.2
  249.8 3.4 copy-start.2
  256.9 3.4 copy-start.2
  268.4 3.4 copy-start.2
  275.5 3.4 copy-start.2
  316.2 77.7 %copy-start.1 = (bf16[8192,64]{0,1:T(8,128)(2,1)S(1)}, bf16[8192,64]{0,1:T(8,128)(2,1)}, u32[]{:S(2)}) copy-start(bf16[8192,64]{0,1:T(8,128)(2,1)} %param.14) | copy-start | bytes 3145732
  324.0 69.9 %reduce-scatter.5.cloned.1.call-start = ((), (), s32[]{:S(2)}) async-start(), calls=%async_computation.6 | async-start | bytes 1310720 | tf_op jit(solution)/shard_map/reduce_scatter | solution.py:68
Sparse Core Ops, SparseCore 0:
  324.2 44.0 reduce-scatter.2
  370.8 23.0 reduce-scatter.4
